TPU v7x, 32 devices: a whole 2x2x4 slice. The times are simulated.
32 devices in a mesh: dp: 8 (over y, x, core), mp: 4 (over z).
Axes of the slice: x: 2, y: 2, z: 4, core: 2. Of those that a mesh axis runs over, the one named last changes fastest.
Arguments:
- inputs: bfloat16 [32768, 768], P(('dp', 'mp')), may hold values from -6 to 6
- lengths: int32 [32], P(('dp', 'mp')), may hold values from 102 to 1024, as said below
- attn_qkv: bfloat16 [1, 768, 2304], P(None, ('dp', 'mp')), may hold values from -0.21875 to 0.21875
- attn_proj: bfloat16 [1, 768, 768], P(None, ('dp', 'mp')), may hold values from -1.75 to 1.75
- mlp_in: bfloat16 [1, 768, 3072], P(None, 'dp', 'mp'), may hold values from -0.21875 to 0.21875
- mlp_out: bfloat16 [1, 3072, 768], P(None, 'mp', 'dp'), may hold values from -0.109375 to 0.109375
- norm_gain: bfloat16 [1, 2, 768], P(None, None, ('dp', 'mp')), may hold values from 0.099609375 to 1.8984375
- norm_bias: bfloat16 [1, 2, 768], P(None, None, ('dp', 'mp')), may hold values from -1.5 to 1.5
- cotangent: bfloat16 [32768, 768], P(('dp', 'mp')), may hold values from -6 to 6
Outputs:
- outputs: bfloat16 [32768, 768], P(('dp', 'mp'))
- input_grad: float32 [32768, 768], P(('dp', 'mp'))
- qkv_grad: float32 [1, 768, 2304], P(None, ('dp', 'mp'))
- proj_grad: float32 [1, 768, 768], P(None, ('dp', 'mp'))
- mlp_in_grad: float32 [1, 768, 3072], P(None, 'dp', 'mp')
- mlp_out_grad: float32 [1, 3072, 768], P(None, 'mp', 'dp')
- gain_grad: float32 [1, 2, 768], P(None, None, ('dp', 'mp'))
- bias_grad: float32 [1, 2, 768], P(None, None, ('dp', 'mp'))
Inputs may be any that keep to these rules, and one draw needn't show every extreme that they name: `lengths`: the true patch count of each clip; slots at or beyond it are padding. Some clip has 1024 patches and some has 102.
All inputs are finite; a program needn't handle non-finite values.
Results may differ from a plain program's by a relative error of at most 0.011.
Values may be sent and summed in bfloat16 or wider, within the bound.
A program may use at most 320 MiB of HBM per device.

v0:
```python
from functools import partial
import math

import jax
import jax.numpy as jnp
from jax import lax
from jax.sharding import PartitionSpec as P

D = 768
HEADS = 12
HEAD_DIM = 64
LAYERS = 1


def layer_norm(values, scales, shifts):
    centre = values - jnp.mean(values, axis=-1, keepdims=True)
    spread = jnp.mean(centre * centre, axis=-1, keepdims=True)
    return centre * lax.rsqrt(spread + 1e-06) * scales + shifts


def gelu_exact(values):
    return jax.nn.gelu(values, approximate=False)


def collect(qkv_part, proj_part, gain_part, shift_part, in_part, out_part):
    qkv_mid, proj_mid, gain_mid, shift_mid, in_mid, out_mid = (
        lax.all_gather(qkv_part, "mp", axis=0, tiled=True),
        lax.all_gather(proj_part, "mp", axis=0, tiled=True),
        lax.all_gather(gain_part, "mp", axis=1, tiled=True),
        lax.all_gather(shift_part, "mp", axis=1, tiled=True),
        lax.all_gather(in_part, "mp", axis=1, tiled=True),
        lax.all_gather(out_part, "mp", axis=0, tiled=True),
    )
    return (
        lax.all_gather(qkv_mid, "dp", axis=0, tiled=True),
        lax.all_gather(proj_mid, "dp", axis=0, tiled=True),
        lax.all_gather(gain_mid, "dp", axis=1, tiled=True),
        lax.all_gather(shift_mid, "dp", axis=1, tiled=True),
        lax.all_gather(in_mid, "dp", axis=0, tiled=True),
        lax.all_gather(out_mid, "dp", axis=1, tiled=True),
    )


def spread_sums(qkv_whole, proj_whole, gain_whole, shift_whole, in_whole, out_whole):
    qkv_mid, proj_mid, gain_mid, shift_mid, in_mid, out_mid = (
        lax.psum_scatter(qkv_whole, "dp", scatter_dimension=0, tiled=True),
        lax.psum_scatter(proj_whole, "dp", scatter_dimension=0, tiled=True),
        lax.psum_scatter(gain_whole, "dp", scatter_dimension=1, tiled=True),
        lax.psum_scatter(shift_whole, "dp", scatter_dimension=1, tiled=True),
        lax.psum_scatter(in_whole, "dp", scatter_dimension=0, tiled=True),
        lax.psum_scatter(out_whole, "dp", scatter_dimension=1, tiled=True),
    )
    return (
        lax.psum_scatter(qkv_mid, "mp", scatter_dimension=0, tiled=True),
        lax.psum_scatter(proj_mid, "mp", scatter_dimension=0, tiled=True),
        lax.psum_scatter(gain_mid, "mp", scatter_dimension=1, tiled=True),
        lax.psum_scatter(shift_mid, "mp", scatter_dimension=1, tiled=True),
        lax.psum_scatter(in_mid, "mp", scatter_dimension=1, tiled=True),
        lax.psum_scatter(out_mid, "mp", scatter_dimension=0, tiled=True),
    )


def split_heads(packed_clip, block):
    slots = packed_clip.shape[0]
    queries = packed_clip[:, :D].reshape(slots // block, block, HEADS, HEAD_DIM)
    keys = packed_clip[:, D : 2 * D].reshape(slots, HEADS, HEAD_DIM)
    values = packed_clip[:, 2 * D :].reshape(slots, HEADS, HEAD_DIM)
    return (queries, keys, values)


def attend_forward(element, block, scale):
    packed_clip, length = element
    slots = packed_clip.shape[0]
    queries, keys, values = split_heads(packed_clip, block)
    valid = lax.iota(jnp.int32, slots) < length

    def one_block(query_block):
        scores = (
            jnp.einsum("qhd,khd->hqk", query_block, keys, preferred_element_type=jnp.float32)
            * scale
        )
        scores = jnp.where(valid[None, None, :], scores, -1e30)
        biggest = jnp.max(scores, axis=-1, keepdims=True)
        powers = jnp.exp(scores - biggest)
        totals = jnp.sum(powers, axis=-1, keepdims=True)
        weights = (powers / totals).astype(jnp.bfloat16)
        mixed = jnp.einsum("hqk,khd->qhd", weights, values, preferred_element_type=jnp.float32)
        return (mixed.astype(jnp.bfloat16).reshape(block, D), (biggest + jnp.log(totals))[:, :, 0])

    mixed, logsum = lax.map(one_block, queries)
    return (mixed.reshape(slots, D), logsum)


def attend_backward(element, block, scale):
    packed_clip, length, logsum, grad_clip = element
    slots = packed_clip.shape[0]
    queries, keys, values = split_heads(packed_clip, block)
    valid = lax.iota(jnp.int32, slots) < length
    grad_blocks = grad_clip.reshape(slots // block, block, HEADS, HEAD_DIM)

    def one_block(carried, element_block):
        key_grad, value_grad = carried
        query_block, grad_block, logsum_block = element_block
        scores = (
            jnp.einsum("qhd,khd->hqk", query_block, keys, preferred_element_type=jnp.float32)
            * scale
        )
        scores = jnp.where(valid[None, None, :], scores, -1e30)
        probs = jnp.exp(scores - logsum_block[:, :, None])
        prob_grad = jnp.einsum(
            "qhd,khd->hqk", grad_block, values, preferred_element_type=jnp.float32
        )
        score_grad = (
            probs * (prob_grad - jnp.sum(probs * prob_grad, axis=-1, keepdims=True))
        ).astype(jnp.bfloat16)
        query_grad = (
            jnp.einsum("hqk,khd->qhd", score_grad, keys, preferred_element_type=jnp.float32) * scale
        )
        key_grad = (
            key_grad
            + jnp.einsum(
                "hqk,qhd->khd", score_grad, query_block, preferred_element_type=jnp.float32
            )
            * scale
        )
        value_grad = value_grad + jnp.einsum(
            "hqk,qhd->khd",
            probs.astype(jnp.bfloat16),
            grad_block,
            preferred_element_type=jnp.float32,
        )
        return ((key_grad, value_grad), query_grad.reshape(block, D))

    zeros = jnp.zeros((slots, HEADS, HEAD_DIM), jnp.float32)
    (key_grad, value_grad), query_grad = lax.scan(
        one_block, (zeros, zeros), (queries, grad_blocks, logsum)
    )
    return jnp.concatenate(
        [query_grad.reshape(slots, D), key_grad.reshape(slots, D), value_grad.reshape(slots, D)],
        axis=1,
    )


def per_device(
    inputs, lengths, attn_qkv, attn_proj, mlp_in, mlp_out, norm_gain, norm_bias, cotangent
):
    clips_here = lengths.shape[0]
    row_count = inputs.shape[0]
    slots = row_count // clips_here
    block = min(512, slots)
    scale = 1.0 / math.sqrt(HEAD_DIM)
    forward_block = partial(attend_forward, block=block, scale=scale)
    backward_block = partial(attend_backward, block=block, scale=scale)
    hidden = inputs.astype(jnp.float32)
    layer_index = 0
    qkv_w, proj_w, gain_w, shift_w, in_w, out_w = collect(
        attn_qkv[layer_index],
        attn_proj[layer_index],
        norm_gain[layer_index],
        norm_bias[layer_index],
        mlp_in[layer_index],
        mlp_out[layer_index],
    )
    gain_f = gain_w.astype(jnp.float32)
    shift_f = shift_w.astype(jnp.float32)
    normed = layer_norm(hidden, gain_f[0], shift_f[0]).astype(jnp.bfloat16)
    packed = jnp.dot(normed, qkv_w, preferred_element_type=jnp.float32).astype(jnp.bfloat16)
    mixed, logsum = lax.map(forward_block, (packed.reshape(clips_here, slots, 3 * D), lengths))
    mixed = mixed.reshape(row_count, D)
    middle = hidden + jnp.dot(mixed, proj_w, preferred_element_type=jnp.float32)
    second = layer_norm(middle, gain_f[1], shift_f[1]).astype(jnp.bfloat16)
    expanded = jnp.dot(second, in_w, preferred_element_type=jnp.float32)
    activated = gelu_exact(expanded).astype(jnp.bfloat16)
    stored = [
        (
            hidden,
            normed,
            packed,
            logsum,
            mixed,
            middle,
            second,
            expanded,
            activated,
            qkv_w,
            proj_w,
            gain_f,
            shift_f,
            in_w,
            out_w,
        )
    ]
    hidden = middle + jnp.dot(activated, out_w, preferred_element_type=jnp.float32)
    outputs = hidden.astype(jnp.bfloat16)
    valid_rows = (lax.iota(jnp.int32, slots)[None, :] < lengths[:, None]).reshape(-1)
    upstream = jnp.where(valid_rows[:, None], cotangent.astype(jnp.float32), 0.0)
    shares = [None] * LAYERS
    for layer_index in reversed(range(LAYERS)):
        (
            hidden_in,
            normed,
            packed,
            logsum,
            mixed,
            middle,
            second,
            expanded,
            activated,
            qkv_w,
            proj_w,
            gain_f,
            shift_f,
            in_w,
            out_w,
        ) = stored[layer_index]
        branch_low = upstream.astype(jnp.bfloat16)
        out_w_grad = jnp.dot(activated.T, branch_low, preferred_element_type=jnp.float32)
        act_grad = jnp.dot(branch_low, out_w.T, preferred_element_type=jnp.float32)
        unused, gelu_pull = jax.vjp(gelu_exact, expanded)
        exp_grad = gelu_pull(act_grad)[0].astype(jnp.bfloat16)
        in_w_grad = jnp.dot(second.T, exp_grad, preferred_element_type=jnp.float32)
        second_grad = jnp.dot(exp_grad, in_w.T, preferred_element_type=jnp.float32)
        unused, norm_pull = jax.vjp(layer_norm, middle, gain_f[1], shift_f[1])
        middle_part, gain_two, shift_two = norm_pull(second_grad)
        middle_grad = upstream + middle_part
        attn_low = middle_grad.astype(jnp.bfloat16)
        proj_w_grad = jnp.dot(mixed.T, attn_low, preferred_element_type=jnp.float32)
        mixed_grad = jnp.dot(attn_low, proj_w.T, preferred_element_type=jnp.float32).astype(
            jnp.bfloat16
        )
        packed_grad = lax.map(
            backward_block,
            (
                packed.reshape(clips_here, slots, 3 * D),
                lengths,
                logsum,
                mixed_grad.reshape(clips_here, slots, D),
            ),
        )
        packed_grad = packed_grad.reshape(row_count, 3 * D).astype(jnp.bfloat16)
        qkv_w_grad = jnp.dot(normed.T, packed_grad, preferred_element_type=jnp.float32)
        normed_grad = jnp.dot(packed_grad, qkv_w.T, preferred_element_type=jnp.float32)
        unused, first_pull = jax.vjp(layer_norm, hidden_in, gain_f[0], shift_f[0])
        input_part, gain_one, shift_one = first_pull(normed_grad)
        upstream = middle_grad + input_part
        shares[layer_index] = spread_sums(
            qkv_w_grad,
            proj_w_grad,
            jnp.stack([gain_one, gain_two]),
            jnp.stack([shift_one, shift_two]),
            in_w_grad,
            out_w_grad,
        )
    qkv_grad = jnp.stack([share[0] for share in shares])
    proj_grad = jnp.stack([share[1] for share in shares])
    gain_grad = jnp.stack([share[2] for share in shares])
    bias_grad = jnp.stack([share[3] for share in shares])
    mlp_in_grad = jnp.stack([share[4] for share in shares])
    mlp_out_grad = jnp.stack([share[5] for share in shares])
    return (outputs, upstream, qkv_grad, proj_grad, mlp_in_grad, mlp_out_grad, gain_grad, bias_grad)


def solution(mesh):
    return jax.shard_map(
        per_device,
        mesh=mesh,
        in_specs=(
            P(("dp", "mp"), None),
            P(("dp", "mp")),
            P(None, ("dp", "mp"), None),
            P(None, ("dp", "mp"), None),
            P(None, "dp", "mp"),
            P(None, "mp", "dp"),
            P(None, None, ("dp", "mp")),
            P(None, None, ("dp", "mp")),
            P(("dp", "mp"), None),
        ),
        out_specs=(
            P(("dp", "mp"), None),
            P(("dp", "mp"), None),
            P(None, ("dp", "mp"), None),
            P(None, ("dp", "mp"), None),
            P(None, "dp", "mp"),
            P(None, "mp", "dp"),
            P(None, None, ("dp", "mp")),
            P(None, None, ("dp", "mp")),
        ),
        check_vma=False,
    )
```

profile of v0, /device:TPU:0, one launch (start us, length us, event | category | flops | bytes accessed | tf_op | source)
XLA Modules:
  0.0 939.8 jit_solution(8329434364469881361)
XLA Ops:
  7.2 18.5 %all-gather.4 = bf16[1,96,2304]{2,1,0:T(8,128)(2,1)} all-gather(bf16[1,24,2304]{2,1,0:T(8,128)(2,1)} %param.15), channel_id=6, replica_groups=mesh['dp'=8,'mp'=4] {'mp'}, dimensions={1}, use_global_device_ids=true | all-gather | bytes 552960 | tf_op jit(solution)/shard_map/all_gather | solution.py:27
  25.8 14.5 %all-gather.6 = bf16[1,96,768]{2,1,0:T(8,128)(2,1)} all-gather(bf16[1,24,768]{2,1,0:T(8,128)(2,1)} %param.16), channel_id=8, replica_groups=mesh['dp'=8,'mp'=4] {'mp'}, dimensions={1}, use_global_device_ids=true | all-gather | bytes 184320 | tf_op jit(solution)/shard_map/all_gather | solution.py:28
  40.3 17.9 %all-gather.8 = bf16[1,96,3072]{2,1,0:T(8,128)(2,1)} all-gather(bf16[1,96,768]{2,1,0:T(8,128)(2,1)} %param.17), channel_id=10, replica_groups=mesh['dp'=8,'mp'=4] {'mp'}, dimensions={2}, use_global_device_ids=true | all-gather | bytes 737280 | tf_op jit(solution)/shard_map/all_gather | solution.py:31
  58.3 16.3 %all-gather.10 = bf16[1,3072,96]{1,2,0:T(8,128)(2,1)} all-gather(bf16[1,768,96]{1,2,0:T(8,128)(2,1)} %param.18), channel_id=12, replica_groups=mesh['dp'=8,'mp'=4] {'mp'}, dimensions={1}, use_global_device_ids=true | all-gather | bytes 737280 | tf_op jit(solution)/shard_map/all_gather | solution.py:32
  76.1 13.1 %all-gather.2 = bf16[1,2,96]{1,0,2:T(2,128)(2,1)S(1)} all-gather(bf16[1,2,24]{1,0,2:T(2,128)(2,1)S(1)} %copy.97), channel_id=4, replica_groups=mesh['dp'=8,'mp'=4] {'mp'}, dimensions={2}, use_global_device_ids=true | all-gather | bytes 480 | tf_op jit(solution)/shard_map/all_gather | solution.py:30
  89.1 13.1 %all-gather = bf16[1,2,96]{1,0,2:T(2,128)(2,1)S(1)} all-gather(bf16[1,2,24]{1,0,2:T(2,128)(2,1)S(1)} %copy.96), channel_id=2, replica_groups=mesh['dp'=8,'mp'=4] {'mp'}, dimensions={2}, use_global_device_ids=true | all-gather | bytes 480 | tf_op jit(solution)/shard_map/all_gather | solution.py:29
  102.2 9.6 %all-gather.1 = bf16[1,2,768]{1,0,2:T(2,128)(2,1)S(1)} all-gather(bf16[1,2,96]{1,0,2:T(2,128)(2,1)S(1)} %all-gather), channel_id=3, replica_groups=mesh['dp'=8,'mp'=4] {'dp'}, dimensions={2}, use_global_device_ids=true | all-gather | bytes 3456 | tf_op jit(solution)/shard_map/all_gather | solution.py:37
  112.2 4.6 slice_reduce_fusion.1
  116.8 10.6 %all-gather.3 = bf16[1,2,768]{1,0,2:T(2,128)(2,1)S(1)} all-gather(bf16[1,2,96]{1,0,2:T(2,128)(2,1)S(1)} %all-gather.2), channel_id=5, replica_groups=mesh['dp'=8,'mp'=4] {'dp'}, dimensions={2}, use_global_device_ids=true | all-gather | bytes 3456 | tf_op jit(solution)/shard_map/all_gather | solution.py:38
  127.8 4.6 slice_reduce_fusion
  137.1 6.7 convolution_convert_fusion
  150.2 4.0 reshape.181
  155.9 77.8 %while.46 = (s32[]{:T(128)}, bf16[2,512,768]{2,1,0:T(8,128)(2,1)}, f32[2,12,512]{2,1,0:T(8,128)S(1)}, bf16[2,512,12,64]{1,3,2,0:T(8,128)(2,1)S(1)}, bf16[1024,12...) while((s32[]{:T(128)}, bf16[2,512,768]{2,1,0:T(8,128)(2,1)}, ...), condition=%wide.region_5.6_spmd.clone, body=%wide.region_2.5_spmd.clone.sunk | while | flops 1686498304 | bytes 89878664 | solution.py:90
  156.6 10.3 %fusion.122 = (f32[12,512]{1,0:T(8,128)S(1)}, f32[12,512,1024]{2,1,0:T(8,128)}) fusion(pred[1024]{0:T(1024)(128)(4,1)S(1)} %iota_compare_fusion.5, bf16[1024,12,64]{0,2,1:T(8,128)(2,1)S(1)} %get-tuple-element.512, bf16[2,512,12,64]{1,3,2,0:T(8,128)(2,1)S(1)} %get-tuple-element.511, s32[]{:T(128)S(6)} %copy.152), kind=kOutput, calls=%fused_computation.5.clone.1 | convolution fusion | flops 824174592 | bytes 27550724 | tf_op jit(solution)/shard_map/while/body/eval_jaxpr/while/body/eval_jaxpr/qhd,khd->hqk/dot_general | solution.py:79
  166.9 11.4 %fusion.123 = f32[12,512]{1,0:T(8,128)S(1)} fusion(f32[12,512,1024]{2,1,0:T(8,128)} %get-tuple-element.478, f32[12,512]{1,0:T(8,128)S(1)} %get-tuple-element.479, pred[1024]{0:T(1024)(128)(4,1)S(1)} %iota_compare_fusion.5), kind=kLoop, calls=%fused_computation.6.clone.1 | loop fusion | flops 25159680 | bytes 25216000 | tf_op jit(solution)/shard_map/while/body/eval_jaxpr/while/body/eval_jaxpr/reduce_sum | solution.py:85
  178.3 12.0 %fusion.124 = bf16[12,512,64]{1,2,0:T(8,128)(2,1)} fusion(bf16[1024,12,64]{0,2,1:T(8,128)(2,1)S(1)} %copy-done, f32[12,512,1024]{2,1,0:T(8,128)} %get-tuple-element.478, f32[12,512]{1,0:T(8,128)S(1)} %fusion.123, f32[12,512]{1,0:T(8,128)S(1)} %get-tuple-element.479, pred[1024]{0:T(1024)(128)(4,1)S(1)} %iota_compare_fusion.5), kind=kOutput, calls=%fused_computation.8.clone.1 | convolution fusion | flops 837156864 | bytes 27575296 | tf_op jit(solution)/shard_map/while/body/eval_jaxpr/while/body/eval_jaxpr/hqk,khd->qhd/dot_general | solution.py:87
  190.4 2.3 copy.144
  195.4 10.1 %fusion.122 = (f32[12,512]{1,0:T(8,128)S(1)}, f32[12,512,1024]{2,1,0:T(8,128)}) fusion(pred[1024]{0:T(1024)(128)(4,1)S(1)} %iota_compare_fusion.5, bf16[1024,12,64]{0,2,1:T(8,128)(2,1)S(1)} %get-tuple-element.512, bf16[2,512,12,64]{1,3,2,0:T(8,128)(2,1)S(1)} %get-tuple-element.511, s32[]{:T(128)S(6)} %copy.152), kind=kOutput, calls=%fused_computation.5.clone.1 | convolution fusion | flops 824174592 | bytes 27550724 | tf_op jit(solution)/shard_map/while/body/eval_jaxpr/while/body/eval_jaxpr/qhd,khd->hqk/dot_general | solution.py:79
  205.5 11.3 %fusion.123 = f32[12,512]{1,0:T(8,128)S(1)} fusion(f32[12,512,1024]{2,1,0:T(8,128)} %get-tuple-element.478, f32[12,512]{1,0:T(8,128)S(1)} %get-tuple-element.479, pred[1024]{0:T(1024)(128)(4,1)S(1)} %iota_compare_fusion.5), kind=kLoop, calls=%fused_computation.6.clone.1 | loop fusion | flops 25159680 | bytes 25216000 | tf_op jit(solution)/shard_map/while/body/eval_jaxpr/while/body/eval_jaxpr/reduce_sum | solution.py:85
  216.9 12.1 %fusion.124 = bf16[12,512,64]{1,2,0:T(8,128)(2,1)} fusion(bf16[1024,12,64]{0,2,1:T(8,128)(2,1)S(1)} %copy-done, f32[12,512,1024]{2,1,0:T(8,128)} %get-tuple-element.478, f32[12,512]{1,0:T(8,128)S(1)} %fusion.123, f32[12,512]{1,0:T(8,128)S(1)} %get-tuple-element.479, pred[1024]{0:T(1024)(128)(4,1)S(1)} %iota_compare_fusion.5), kind=kOutput, calls=%fused_computation.8.clone.1 | convolution fusion | flops 837156864 | bytes 27575296 | tf_op jit(solution)/shard_map/while/body/eval_jaxpr/while/body/eval_jaxpr/hqk,khd->qhd/dot_general | solution.py:87
  233.7 3.8 fusion.86
  239.7 37.3 %multiply_convert_fusion.1 = (bf16[1024,3072]{1,0:T(8,128)(2,1)}, f32[1024,3072]{1,0:T(8,128)}, f32[1024,3072]{1,0:T(8,128)}) fusion(bf16[1,768,3072]{2,1,0:T(8,128)(2,1)} %all-gather.21.cloned.1.call-done, f32[1024,768]{0,1:T(8,128)} %copy-done.4, f32[768]{0:T(1024)S(1)} %copy-done.31, f32[768]{0:T(1024)S(1)} %copy-done.26, f32[1024]{0:T(1024)S(1)} %fusion.75, ...), kind=kOutput, calls=%fused_computation.49 | convolution fusion | flops 5040242688 | bytes 39335936 | tf_op jit(solution)/shard_map/dot_general | solution.py:172
  277.0 18.9 %add_convert_fusion = bf16[1024,3072]{1,0:T(8,128)(2,1)} fusion(f32[1024,3072]{1,0:T(8,128)} %get-tuple-element.363, f32[1024,3072]{1,0:T(8,128)} %get-tuple-element.373, bf16[1,3072,768]{1,2,0:T(8,128)(2,1)} %all-gather.23.cloned.1.call-done, bf16[1024,768]{0,1:T(8,128)(2,1)} %copy.104, pred[1024]{0:T(1024)(128)(4,1)S(1)} %copy-done.35), kind=kOutput, calls=%fused_computation.48 | convolution fusion | flops 4878237696 | bytes 37749760 | tf_op jit(solution)/shard_map/dot_general | solution.py:218
  295.9 9.0 fusion.87
  304.9 3.5 copy.105
  308.4 4.5 multiply_reduce_fusion.1
  316.7 2.8 fusion.89
  319.6 4.3 convolution_convert_fusion.1
  323.9 2.6 copy.106
  326.5 3.8 reshape.185
  330.4 2.9 copy.108
  333.3 173.5 %while.47 = (s32[]{:T(128)}, f32[1024,12,64]{0,2,1:T(8,128)}, f32[1024,12,64]{0,2,1:T(8,128)}, bf16[2,512,768]{2,1,0:T(8,128)(2,1)}, bf16[2,512,12,64]{1,3,2,0:T...) while((s32[]{:T(128)}, f32[1024,12,64]{0,2,1:T(8,128)}, ...), condition=%wide.region_12.13_spmd.clone, body=%wide.region_10.12_spmd.clone.sunk | while | flops 4125617152 | bytes 219599024 | solution.py:135
  334.4 11.0 %fusion.134 = f32[12,512,1024]{2,1,0:T(8,128)} fusion(bf16[1024,12,64]{0,2,1:T(8,128)(2,1)S(1)} %get-tuple-element.545, bf16[2,512,12,64]{1,3,2,0:T(8,128)(2,1)S(1)} %get-tuple-element.544, s32[]{:T(128)S(6)} %copy.162), kind=kOutput, calls=%fused_computation.31.clone.1 | convolution fusion | flops 805306368 | bytes 27525124 | tf_op jit(solution)/shard_map/while/body/eval_jaxpr/while/body/eval_jaxpr/qhd,khd->hqk/dot_general | solution.py:105
  345.5 13.0 %bitcast_add_fusion.5 = f32[1024,12,64]{0,2,1:T(8,128)} fusion(f32[1024,12,64]{0,2,1:T(8,128)} %get-tuple-element.530, f32[12,512,1024]{2,1,0:T(8,128)} %fusion.134, f32[12,512]{1,0:T(8,128)S(1)} %dynamic-slice_bitcast_fusion.4, pred[1024]{0:T(1024)(128)(4,1)S(1)} %iota_compare_fusion.6, pred[]{:T(512)S(6)} %compare.3, ...), kind=kOutput, calls=%fused_computation.24.clone.1 | convolution fusion | flops 832045056 | bytes 32277508 | tf_op jit(solution)/shard_map/while/body/eval_jaxpr/while/body/eval_jaxpr/hqk,qhd->khd/dot_general | solution.py:126
  358.5 17.7 %multiply_reduce_fusion.5 = (f32[12,512]{1,0:T(8,128)S(1)}, f32[12,512,1024]{2,1,0:T(8,128)}) fusion(f32[12,512,1024]{2,1,0:T(8,128)} %fusion.134, f32[12,512]{1,0:T(8,128)S(1)} %dynamic-slice_bitcast_fusion.4, pred[1024]{0:T(1024)(128)(4,1)S(1)} %iota_compare_fusion.6, bf16[1024,12,64]{0,2,1:T(8,128)(2,1)} %get-tuple-element.548, ...), kind=kOutput, calls=%fused_computation.19.clone.1 | convolution fusion | flops 836757504 | bytes 52741124 | tf_op jit(solution)/shard_map/while/body/eval_jaxpr/while/body/eval_jaxpr/qhd,khd->hqk/dot_general | solution.py:110
  376.2 21.4 %multiply_convert_fusion.3 = bf16[12,512,1024]{2,1,0:T(8,128)(2,1)} fusion(f32[12,512,1024]{2,1,0:T(8,128)} %get-tuple-element.490, f32[12,512,1024]{2,1,0:T(8,128)} %fusion.134, f32[12,512]{1,0:T(8,128)S(1)} %get-tuple-element.491, f32[12,512]{1,0:T(8,128)S(1)} %dynamic-slice_bitcast_fusion.4, pred[1024]{0:T(1024)(128)(4,1)S(1)} %iota_compare_fusion.6), kind=kLoop, calls=%fused_computation.18.clone.1 | loop fusion | flops 37748736 | bytes 62964736 | tf_op jit(solution)/shard_map/while/body/eval_jaxpr/while/body/eval_jaxpr/convert_element_type | solution.py:115
  397.6 9.4 convolution_multiply_fusion.2
  407.0 8.6 bitcast_add_fusion.4
  420.7 10.1 %fusion.134 = f32[12,512,1024]{2,1,0:T(8,128)} fusion(bf16[1024,12,64]{0,2,1:T(8,128)(2,1)S(1)} %get-tuple-element.545, bf16[2,512,12,64]{1,3,2,0:T(8,128)(2,1)S(1)} %get-tuple-element.544, s32[]{:T(128)S(6)} %copy.162), kind=kOutput, calls=%fused_computation.31.clone.1 | convolution fusion | flops 805306368 | bytes 27525124 | tf_op jit(solution)/shard_map/while/body/eval_jaxpr/while/body/eval_jaxpr/qhd,khd->hqk/dot_general | solution.py:105
  430.7 13.8 %bitcast_add_fusion.5 = f32[1024,12,64]{0,2,1:T(8,128)} fusion(f32[1024,12,64]{0,2,1:T(8,128)} %get-tuple-element.530, f32[12,512,1024]{2,1,0:T(8,128)} %fusion.134, f32[12,512]{1,0:T(8,128)S(1)} %dynamic-slice_bitcast_fusion.4, pred[1024]{0:T(1024)(128)(4,1)S(1)} %iota_compare_fusion.6, pred[]{:T(512)S(6)} %compare.3, ...), kind=kOutput, calls=%fused_computation.24.clone.1 | convolution fusion | flops 832045056 | bytes 32277508 | tf_op jit(solution)/shard_map/while/body/eval_jaxpr/while/body/eval_jaxpr/hqk,qhd->khd/dot_general | solution.py:126
  444.6 17.4 %multiply_reduce_fusion.5 = (f32[12,512]{1,0:T(8,128)S(1)}, f32[12,512,1024]{2,1,0:T(8,128)}) fusion(f32[12,512,1024]{2,1,0:T(8,128)} %fusion.134, f32[12,512]{1,0:T(8,128)S(1)} %dynamic-slice_bitcast_fusion.4, pred[1024]{0:T(1024)(128)(4,1)S(1)} %iota_compare_fusion.6, bf16[1024,12,64]{0,2,1:T(8,128)(2,1)} %get-tuple-element.548, ...), kind=kOutput, calls=%fused_computation.19.clone.1 | convolution fusion | flops 836757504 | bytes 52741124 | tf_op jit(solution)/shard_map/while/body/eval_jaxpr/while/body/eval_jaxpr/qhd,khd->hqk/dot_general | solution.py:110
  462.0 21.4 %multiply_convert_fusion.3 = bf16[12,512,1024]{2,1,0:T(8,128)(2,1)} fusion(f32[12,512,1024]{2,1,0:T(8,128)} %get-tuple-element.490, f32[12,512,1024]{2,1,0:T(8,128)} %fusion.134, f32[12,512]{1,0:T(8,128)S(1)} %get-tuple-element.491, f32[12,512]{1,0:T(8,128)S(1)} %dynamic-slice_bitcast_fusion.4, pred[1024]{0:T(1024)(128)(4,1)S(1)} %iota_compare_fusion.6), kind=kLoop, calls=%fused_computation.18.clone.1 | loop fusion | flops 37748736 | bytes 62964736 | tf_op jit(solution)/shard_map/while/body/eval_jaxpr/while/body/eval_jaxpr/convert_element_type | solution.py:115
  483.4 9.4 convolution_multiply_fusion.2
  492.8 9.5 %bitcast_add_fusion.4 = f32[1024,12,64]{0,2,1:T(8,128)} fusion(f32[1024,12,64]{0,2,1:T(8,128)} %get-tuple-element.529, bf16[12,512,1024]{2,1,0:T(8,128)(2,1)} %multiply_convert_fusion.3, pred[]{:T(512)S(6)} %compare.3, bf16[2,512,12,64]{1,3,2,0:T(8,128)(2,1)S(1)} %get-tuple-element.544, s32[]{:T(128)S(6)} %copy.162), kind=kOutput, calls=%fused_computation.25.clone.1 | convolution fusion | flops 807665664 | bytes 19660804 | tf_op jit(solution)/shard_map/while/body/eval_jaxpr/while/body/eval_jaxpr/hqk,qhd->khd/dot_general | solution.py:121
  514.4 9.3 fusion.64
  524.5 10.8 %fusion.82 = f32[768,3072]{1,0:T(8,128)} fusion(bf16[1024,3072]{1,0:T(8,128)(2,1)} %add_convert_fusion, f32[1024,768]{0,1:T(8,128)} %copy-done.4, f32[768]{0:T(1024)S(1)} %copy-done.32, f32[768]{0:T(1024)S(1)} %copy-done.27, f32[1024]{0:T(1024)S(1)} %copy-done.29, f32[1024]{0:T(1024)S(1)} %copy-done.19), kind=kOutput, calls=%fused_computation.130 | convolution fusion | flops 4835770368 | bytes 18888704 | tf_op jit(solution)/shard_map/dot_general | solution.py:221
  536.9 10.6 %fusion.68 = f32[3072,768]{0,1:T(8,128)} fusion(bf16[1024,3072]{1,0:T(8,128)(2,1)} %get-tuple-element.362, bf16[1024,768]{0,1:T(8,128)(2,1)S(1)} %copy-done.10, pred[1024]{0:T(1024)(128)(4,1)S(1)} %copy-done.36), kind=kOutput, calls=%fused_computation.103 | convolution fusion | flops 4834197504 | bytes 17302528 | tf_op jit(solution)/shard_map/dot_general | solution.py:217
  548.2 9.1 fusion.88
  558.4 3.8 copy.112
  562.1 2.6 fusion.62
  568.2 20.9 %reduce-scatter.17.cloned.1.call-done = f32[96,2304]{1,0:T(8,128)} async-done(((f32[768,2304]{1,0:T(8,128)}), f32[96,2304]{1,0:T(8,128)}) %reduce-scatter.17.cloned.1.call-update) | async-done | bytes 884752 | tf_op jit(solution)/shard_map/reduce_scatter | solution.py:46
  589.2 79.9 %reduce-scatter.25.cloned.1.call-done = f32[96,3072]{1,0:T(8,128)} async-done(((f32[768,3072]{1,0:T(8,128)}), f32[96,3072]{1,0:T(8,128)}) %reduce-scatter.25.cloned.1.call-update) | async-done | bytes 1179664 | tf_op jit(solution)/shard_map/reduce_scatter | solution.py:50
  670.4 78.7 %reduce-scatter.29.cloned.1.call-done = f32[3072,96]{0,1:T(8,128)} async-done(((f32[3072,768]{0,1:T(8,128)}), f32[3072,96]{0,1:T(8,128)}) %reduce-scatter.29.cloned.1.call-update) | async-done | bytes 1179664 | tf_op jit(solution)/shard_map/reduce_scatter | solution.py:51
  749.2 10.0 %add_convert_fusion.1 = bf16[1024,768]{0,1:T(8,128)(2,1)} fusion(f32[1024,768]{0,1:T(8,128)} %copy-done.4, bf16[1024,3072]{1,0:T(8,128)(2,1)} %get-tuple-element.362, bf16[1,3072,768]{1,2,0:T(8,128)(2,1)} %all-gather.23.cloned.1.call-done), kind=kOutput, calls=%fused_computation.97 | convolution fusion | flops 4833411072 | bytes 15728640 | tf_op jit(solution)/shard_map/dot_general | solution.py:193
  759.2 2.6 copy.115
  761.7 6.0 add_add_fusion.2
  767.8 3.5 copy.116
  771.3 14.7 %reduce-scatter.35.cloned.1.call-done = f32[96,2]{1,0:T(8,128)} async-done(((f32[768,2]{1,0:T(8,128)}), f32[96,2]{1,0:T(8,128)}) %reduce-scatter.35.cloned.1.call-update) | async-done | bytes 784
  786.9 35.9 %reduce-scatter.33.cloned.1.call-done = f32[96,2]{1,0:T(8,128)} async-done(((f32[768,2]{1,0:T(8,128)}), f32[96,2]{1,0:T(8,128)}) %reduce-scatter.33.cloned.1.call-update) | async-done | bytes 784
  823.7 11.8 %all-reduce.2 = (f32[2,96]{1,0:T(2,128)S(1)}, f32[2,96]{1,0:T(2,128)S(1)}) all-reduce(f32[2,96]{1,0:T(2,128)S(1)} %copy.119, f32[2,96]{1,0:T(2,128)S(1)} %copy.123), channel_id=23, replica_groups=mesh['dp'=8,'mp'=4] {'mp'}, use_global_device_ids=true, to_apply=%region_26.27.clone | all-reduce | flops 384 | bytes 3072
  836.1 9.5 %reduce-scatter.23.cloned.1.call-done = f32[24,768]{1,0:T(8,128)} async-done(((f32[96,768]{1,0:T(8,128)}), f32[24,768]{1,0:T(8,128)}) %reduce-scatter.23.cloned.1.call-update) | async-done | bytes 73744 | tf_op jit(solution)/shard_map/reduce_scatter | solution.py:55
  845.6 25.6 %reduce-scatter.19.cloned.1.call-done = f32[24,2304]{1,0:T(8,128)} async-done(((f32[96,2304]{1,0:T(8,128)}), f32[24,2304]{1,0:T(8,128)}) %reduce-scatter.19.cloned.1.call-update) | async-done | bytes 221200 | tf_op jit(solution)/shard_map/reduce_scatter | solution.py:54
  871.2 31.1 %reduce-scatter.27.cloned.1.call-done = f32[96,768]{1,0:T(8,128)} async-done(((f32[96,3072]{1,0:T(8,128)}), f32[96,768]{1,0:T(8,128)}) %reduce-scatter.27.cloned.1.call-update) | async-done | bytes 294928 | tf_op jit(solution)/shard_map/reduce_scatter | solution.py:58
  902.4 30.7 %reduce-scatter.31.cloned.1.call-done = f32[768,96]{0,1:T(8,128)} async-done(((f32[3072,96]{0,1:T(8,128)}), f32[768,96]{0,1:T(8,128)}) %reduce-scatter.31.cloned.1.call-update) | async-done | bytes 294928 | tf_op jit(solution)/shard_map/reduce_scatter | solution.py:59
  (185 shorter events, 56.5 us)
Async XLA Ops:
  7.2 68.7 %copy-start.38 = (bf16[1,2,24]{2,1,0:T(2,128)(2,1)S(1)}, bf16[1,2,24]{2,1,0:T(2,128)(2,1)}, u32[]{:S(2)}) copy-start(bf16[1,2,24]{2,1,0:T(2,128)(2,1)} %param.19) | copy-start | bytes 292
  7.2 68.8 %copy-start.39 = (bf16[1,2,24]{2,1,0:T(2,128)(2,1)S(1)}, bf16[1,2,24]{2,1,0:T(2,128)(2,1)}, u32[]{:S(2)}) copy-start(bf16[1,2,24]{2,1,0:T(2,128)(2,1)} %param.20) | copy-start | bytes 292
  7.2 129.9 %all-gather.17.cloned.1.call-start = ((), (), s32[]{:S(2)}) async-start(), calls=%async_computation.18 | async-start | bytes 3981312 | tf_op jit(solution)/shard_map/all_gather | solution.py:35
  25.7 208.0 %all-gather.19.cloned.1.call-start = ((), (), s32[]{:S(2)}) async-start(), calls=%async_computation.19 | async-start | bytes 1327104 | tf_op jit(solution)/shard_map/all_gather | solution.py:36
  40.2 199.4 %all-gather.21.cloned.1.call-start = ((), (), s32[]{:S(2)}) async-start(), calls=%async_computation.20 | async-start | bytes 5308416 | tf_op jit(solution)/shard_map/all_gather | solution.py:39
  58.2 74.2 %copy-start.11 = (bf16[1024,768]{1,0:T(8,128)(2,1)S(1)}, bf16[1024,768]{1,0:T(8,128)(2,1)}, u32[]{:S(2)}) copy-start(bf16[1024,768]{1,0:T(8,128)(2,1)} %param.13) | copy-start | bytes 4718596
  58.2 218.8 %all-gather.23.cloned.1.call-start = ((), (), s32[]{:S(2)}) async-start(), calls=%async_computation.21 | async-start | bytes 5308416 | tf_op jit(solution)/shard_map/all_gather | solution.py:40
  74.6 492.9 %reduce-scatter.21.cloned.1.call-start = ((), (), s32[]{:S(2)}) async-start(), calls=%async_computation.12 | async-start | bytes 2654208 | tf_op jit(solution)/shard_map/reduce_scatter | solution.py:47
  116.8 20.3 %copy-start.16 = (f32[768]{0:T(1024)}, f32[768]{0:T(1024)S(1)}, u32[]{:S(2)}) copy-start(f32[768]{0:T(1024)S(1)} %get-tuple-element.321) | copy-start | bytes 9220
  132.4 4.7 copy-start.33
  133.4 3.7 copy-start.1
  133.4 2.0 copy-start.12
  133.7 10.1 %copy-start.14 = (f32[1024]{0:T(1024)}, f32[1024]{0:T(1024)S(1)}, u32[]{:S(2)}) copy-start(f32[1024]{0:T(1024)S(1)} %broadcast_multiply_fusion.1) | copy-start | bytes 12292
  134.1 9.6 %copy-start.24 = (f32[1024]{0:T(1024)}, f32[1024]{0:T(1024)S(1)}, u32[]{:S(2)}) copy-start(f32[1024]{0:T(1024)S(1)} %fusion.61) | copy-start | bytes 12292
  135.4 8.4 copy-start.20
  166.9 11.4 %copy-start = (bf16[1024,12,64]{0,2,1:T(8,128)(2,1)S(1)}, bf16[1024,12,64]{0,2,1:T(8,128)(2,1)}, u32[]{:S(2)}) copy-start(bf16[1024,12,64]{0,2,1:T(8,128)(2,1)} %get-tuple-element.513) | copy-start | bytes 4718596 | tf_op jit(solution)/shard_map/while/body/eval_jaxpr/while
  205.5 11.3 %copy-start = (bf16[1024,12,64]{0,2,1:T(8,128)(2,1)S(1)}, bf16[1024,12,64]{0,2,1:T(8,128)(2,1)}, u32[]{:S(2)}) copy-start(bf16[1024,12,64]{0,2,1:T(8,128)(2,1)} %get-tuple-element.513) | copy-start | bytes 4718596 | tf_op jit(solution)/shard_map/while/body/eval_jaxpr/while
  237.5 1.7 copy-start.4
  237.6 2.1 copy-start.26
  237.6 2.1 copy-start.31
  237.6 75.4 %copy-start.18 = (f32[1024]{0:T(1024)}, f32[1024]{0:T(1024)S(1)}, u32[]{:S(2)}) copy-start(f32[1024]{0:T(1024)S(1)} %broadcast_multiply_fusion) | copy-start | bytes 12292
  239.6 73.3 %copy-start.28 = (f32[1024]{0:T(1024)}, f32[1024]{0:T(1024)S(1)}, u32[]{:S(2)}) copy-start(f32[1024]{0:T(1024)S(1)} %fusion.75) | copy-start | bytes 12292
  239.7 37.3 %copy-start.35 = (pred[1024]{0:T(1024)(128)(4,1)S(1)}, pred[1024]{0:T(1024)(128)(4,1)}, u32[]{:S(2)}) copy-start(pred[1024]{0:T(1024)(128)(4,1)} %iota_compare_fusion.2) | copy-start | bytes 3076
  277.0 18.9 %copy-start.40 = (bf16[1,768,3072]{2,1,0:T(8,128)(2,1)S(1)}, bf16[1,768,3072]{2,1,0:T(8,128)(2,1)}, u32[]{:S(2)}) copy-start(bf16[1,768,3072]{2,1,0:T(8,128)(2,1)} %all-gather.21.cloned.1.call-done) | copy-start | bytes 14155780
  308.4 4.5 copy-start.5
  308.4 4.7 copy-start.7
  313.1 1.4 copy-start.9
  313.9 1.7 copy-start.6
  313.9 1.7 copy-start.22
  314.5 2.2 copy-start.41
  315.6 1.2 copy-start.13
  333.3 255.8 %reduce-scatter.17.cloned.1.call-start = ((), (), s32[]{:S(2)}) async-start(), calls=%async_computation.10 | async-start | bytes 7962624 | tf_op jit(solution)/shard_map/reduce_scatter | solution.py:46
  334.4 11.0 %copy-start.8 = (bf16[2,512,12,64]{1,3,2,0:T(8,128)(2,1)S(1)}, bf16[2,512,12,64]{1,3,2,0:T(8,128)(2,1)}, u32[]{:S(2)}) copy-start(bf16[2,512,12,64]{1,3,2,0:T(8,128)(2,1)} %get-tuple-element.547) | copy-start | bytes 4718596 | tf_op jit(solution)/shard_map/while/body/eval_jaxpr/while
  420.6 10.1 %copy-start.8 = (bf16[2,512,12,64]{1,3,2,0:T(8,128)(2,1)S(1)}, bf16[2,512,12,64]{1,3,2,0:T(8,128)(2,1)}, u32[]{:S(2)}) copy-start(bf16[2,512,12,64]{1,3,2,0:T(8,128)(2,1)} %get-tuple-element.547) | copy-start | bytes 4718596 | tf_op jit(solution)/shard_map/while/body/eval_jaxpr/while
  510.5 3.8 copy-start.2
  510.5 3.8 copy-start.15
  510.5 3.8 copy-start.17
  510.6 3.8 copy-start.21
  510.6 3.9 copy-start.34
  523.8 0.7 copy-start.19
  523.8 0.7 copy-start.27
  523.8 0.7 copy-start.29
  523.8 0.7 copy-start.32
  523.8 145.3 %reduce-scatter.25.cloned.1.call-start = ((), (), s32[]{:S(2)}) async-start(), calls=%async_computation.14 | async-start | bytes 10616832 | tf_op jit(solution)/shard_map/reduce_scatter | solution.py:50
  535.3 1.6 copy-start.10
  535.3 1.6 copy-start.36
  535.3 213.8 %reduce-scatter.29.cloned.1.call-start = ((), (), s32[]{:S(2)}) async-start(), calls=%async_computation.16 | async-start | bytes 10616832 | tf_op jit(solution)/shard_map/reduce_scatter | solution.py:51
  547.5 0.7 copy-start.37
  547.5 0.7 copy-start.30
  547.5 238.5 %reduce-scatter.35.cloned.1.call-start = ((), (), s32[]{:S(2)}) async-start(), calls=%async_computation.23 | async-start | bytes 442368
  562.1 2.6 copy-start.25
  562.1 2.8 copy-start.3
  565.0 104.2 %copy-start.42 = (u32[32]{0:T(128)S(1)}, u32[32]{0:T(128)}, u32[]{:S(2)}) copy-start(u32[32]{0:T(128)} %constant.158) | copy-start | bytes 388
  566.3 256.5 %reduce-scatter.33.cloned.1.call-start = ((), (), s32[]{:S(2)}) async-start(), calls=%async_computation.22 | async-start | bytes 442368
  567.4 278.2 %reduce-scatter.23.cloned.1.call-start = ((), (), s32[]{:S(2)}) async-start(), calls=%async_computation.13 | async-start | bytes 368640 | tf_op jit(solution)/shard_map/reduce_scatter | solution.py:55
  568.1 303.1 %reduce-scatter.19.cloned.1.call-start = ((), (), s32[]{:S(2)}) async-start(), calls=%async_computation.11 | async-start | bytes 1105920 | tf_op jit(solution)/shard_map/reduce_scatter | solution.py:54
  589.2 313.2 %reduce-scatter.27.cloned.1.call-start = ((), (), s32[]{:S(2)}) async-start(), calls=%async_computation.15 | async-start | bytes 1474560 | tf_op jit(solution)/shard_map/reduce_scatter | solution.py:58
  669.1 263.9 %reduce-scatter.31.cloned.1.call-start = ((), (), s32[]{:S(2)}) async-start(), calls=%async_computation.17 | async-start | bytes 1474560 | tf_op jit(solution)/shard_map/reduce_scatter | solution.py:59
  759.2 2.6 copy-start.23
Sparse Core Ops, SparseCore 0:
  25.8 34.0 all-gather.16
  61.8 24.0 all-gather.18
  87.8 40.2 all-gather.20
  129.8 39.1 all-gather.22
  333.4 42.1 reduce-scatter.20
  523.9 65.1 reduce-scatter.16
  592.6 76.4 reduce-scatter.24
  672.6 76.4 reduce-scatter.28
  752.2 33.8 reduce-scatter.34
  789.0 33.8 reduce-scatter.32
  825.7 19.8 reduce-scatter.22
  848.3 22.8 reduce-scatter.18
  874.1 28.2 reduce-scatter.26
  905.1 27.8 reduce-scatter.30
where the time goes:
time: 949 us; the launch traced here: 940 us
  waiting for transfers between devices  328 us (35%)
  matrix products  297 us (31%)
  blocking collectives  125 us (13%)
  other arithmetic  91 us (10%)
  local copies, waits for them, and re-layouts  80.9 us (9%)
  between operations  16 us (2%)
    reduce_scatter x1, waiting for transfers between devices, spread_sums(): lax.psum_scatter(in_whole, 'dp', scatter_dimension=0, tiled=True)  79.9 us
    reduce_scatter x1, waiting for transfers between devices, spread_sums(): lax.psum_scatter(out_whole, 'dp', scatter_dimension=1, tiled=True)  78.7 us
    unnamed x16, waiting for transfers between devices  51.5 us
    convert_element_type x2, other arithmetic, one_block(): score_grad = (probs * (prob_grad - jnp.sum(probs * prob_grad, axis=-1, ke...  42.9 us
    dot_general x4, matrix products, one_block(): jnp.einsum('qhd,khd->hqk', query_block, keys, preferred_element_type=jnp....  41.5 us
    dot_general x1, matrix products, per_device(): expanded = jnp.dot(second, in_w, preferred_element_type=jnp.float32)  37.3 us
    dot_general x2, matrix products, one_block(): jnp.einsum('qhd,khd->hqk', grad_block, values, preferred_element_type=jnp...  35.1 us
    reduce_scatter x1, waiting for transfers between devices, spread_sums(): lax.psum_scatter(in_mid, 'mp', scatter_dimension=1, tiled=True)  31.1 us
  transfers between devices with their start and end apart: 14, of which 9 were waited for; matrix products, arithmetic and copies ran while one was open for 43% of the time, Pallas kernels for 0%

commit v1 on v0

v1 whole, which is shorter than its diff:
```python
import functools, math
import jax
import jax.numpy as jnp
from jax.sharding import PartitionSpec as P
from jax import lax
from jax.experimental import pallas as pl
from jax.experimental.pallas import tpu as pltpu
F32=jnp.float32; BF=jnp.bfloat16
HD=64; SCALE=0.125; LOG2E=1.4426950408889634; C=SCALE*LOG2E
NEG=-1e30

def parts3(x):
    hi=x.astype(BF); r=x-hi.astype(F32); mid=r.astype(BF); lo=(r-mid.astype(F32)).astype(BF)
    return hi,mid,lo

def lane_iota(shape): return lax.broadcasted_iota(jnp.int32, shape, len(shape)-1)

def fwd_kernel(len_ref, q_ref, k_ref, v_ref, o_ref, of_ref, lse_ref, *, tq, npair):
    p=pl.program_id(0)
    L=q_ref.shape[0]
    n=len_ref[0]
    lane=lane_iota((L,128))
    k=k_ref[...]; v=v_ref[...]
    kpos=lax.broadcasted_iota(jnp.int32,(L,128),0)
    bias=jnp.where(kpos<n,0.0,NEG).astype(BF)
    zero=jnp.zeros((L,128),BF); one=jnp.ones((L,128),BF)
    @pl.when(p==0)
    def _(): lse_ref[...]=jnp.zeros_like(lse_ref)
    kk=[]; vv=[]
    for h in range(2):
        mine=(lane<64) if h==0 else (lane>=64)
        extra=64*(1-h)
        kk.append(jnp.where(mine,k,jnp.where(lane==extra,bias,zero)))
        vv.append(jnp.where(mine,v,jnp.where(lane==extra,one,zero)))
    lq=lane_iota((tq,128))
    for i in range(L//tq):
        q=q_ref[pl.ds(i*tq,tq),:]
        outs=[]; lses=[]
        for h in range(2):
            mine=(lq<64) if h==0 else (lq>=64)
            extra=64*(1-h)
            qa=jnp.where(mine,q,jnp.where(lq==extra,jnp.ones((tq,128),BF),jnp.zeros((tq,128),BF)))
            s=lax.dot_general(qa,kk[h],(((1,),(1,)),((),())),preferred_element_type=F32)
            m=jnp.max(s,axis=1,keepdims=True)
            e=jnp.exp2(s*C-m*C)
            o=jnp.dot(e.astype(BF),vv[h],preferred_element_type=F32)
            tot=o[:,extra:extra+1]
            outs.append(o/tot); lses.append(m*C+jnp.log2(tot))
        of=jnp.where(lq<64,outs[0],outs[1])
        of_ref[pl.ds(i*tq,tq),:]=of
        o_ref[pl.ds(i*tq,tq),:]=of.astype(BF)
        cur=lse_ref[pl.ds(i*tq,tq),:]
        cur=jnp.where(lq==2*p,lses[0],cur)
        cur=jnp.where(lq==2*p+1,lses[1],cur)
        lse_ref[pl.ds(i*tq,tq),:]=cur

def att_fwd(lengths, packed, tq=256):
    L=packed.shape[0]; D=packed.shape[1]//3; np_=D//128
    spec=lambda off: pl.BlockSpec((L,128),lambda p,off=off:(0,off+p))
    return pl.pallas_call(functools.partial(fwd_kernel,tq=tq,npair=np_),
        grid=(np_,),
        in_specs=[pl.BlockSpec(memory_space=pltpu.SMEM),spec(0),spec(np_),spec(2*np_)],
        out_specs=[pl.BlockSpec((L,128),lambda p:(0,p)),pl.BlockSpec((L,128),lambda p:(0,p)),pl.BlockSpec((L,128),lambda p:(0,0))],
        out_shape=[jax.ShapeDtypeStruct((L,D),BF),jax.ShapeDtypeStruct((L,D),F32),jax.ShapeDtypeStruct((L,128),F32)],
        compiler_params=pltpu.CompilerParams(dimension_semantics=("arbitrary",),vmem_limit_bytes=60*2**20),
    )(lengths,packed,packed,packed)

def bwd_kernel(len_ref, q_ref, k_ref, v_ref, do_ref, of_ref, lse_ref, dq_ref, dk_ref, dv_ref, *, tq):
    p=pl.program_id(0)
    L=q_ref.shape[0]
    n=len_ref[0]
    lane=lane_iota((L,128))
    k=k_ref[...]; v=v_ref[...]
    kpos=lax.broadcasted_iota(jnp.int32,(L,128),0)
    bias=jnp.where(kpos<n,0.0,NEG).astype(BF)
    zero=jnp.zeros((L,128),BF); one=jnp.ones((L,128),BF)
    kk=[]; vv=[]; kz=[]
    for h in range(2):
        mine=(lane<64) if h==0 else (lane>=64)
        b=64*(1-h)
        kk.append(jnp.where(mine,k,jnp.where(lane==b,bias,jnp.where((lane>b)&(lane<b+4),one,zero))))
        vv.append(jnp.where(mine,v,jnp.where((lane>b)&(lane<b+4),one,zero)))
    lq=lane_iota((tq,128))
    dka=[jnp.zeros((L,128),F32)]*2; dva=[jnp.zeros((L,128),F32)]*2
    for i in range(L//tq):
        sl=pl.ds(i*tq,tq)
        q=q_ref[sl,:]; do=do_ref[sl,:]; of=of_ref[sl,:]; lse=lse_ref[sl,:]
        prod=of*do.astype(F32)
        dqs=[]
        for h in range(2):
            mine=(lq<64) if h==0 else (lq>=64)
            b=64*(1-h)
            delta=-jnp.sum(jnp.where(mine,prod,0.0),axis=1,keepdims=True)
            ls=-jnp.sum(jnp.where(lq==2*p+h,lse,0.0),axis=1,keepdims=True)*(1.0/C)
            def aug(x,t,first):
                hi,mid,lo=parts3(jnp.broadcast_to(t,(tq,128)))
                y=jnp.where(lq==b,jnp.full((tq,128),first,BF),jnp.where(lq==b+1,hi,jnp.where(lq==b+2,mid,jnp.where(lq==b+3,lo,jnp.zeros((tq,128),BF)))))
                return jnp.where(mine,x,y)
            qa=aug(q,ls,1.0); da=aug(do,delta,0.0)
            st=lax.dot_general(kk[h],qa,(((1,),(1,)),((),())),preferred_element_type=F32)
            pt=jnp.exp2(st*C)
            dpt=lax.dot_general(vv[h],da,(((1,),(1,)),((),())),preferred_element_type=F32)
            ds=(pt*dpt).astype(BF)
            dva[h]=dva[h]+jnp.dot(pt.astype(BF),do,preferred_element_type=F32)
            dka[h]=dka[h]+jnp.dot(ds,q,preferred_element_type=F32)
            dqs.append(lax.dot_general(ds,k,(((0,),(0,)),((),())),preferred_element_type=F32))
        dq_ref[sl,:]=(jnp.where(lq<64,dqs[0],dqs[1])*SCALE).astype(BF)
    dk_ref[...]=(jnp.where(lane<64,dka[0],dka[1])*SCALE).astype(BF)
    dv_ref[...]=jnp.where(lane<64,dva[0],dva[1]).astype(BF)

def att_bwd(lengths, packed, do, of, lse, tq=256):
    L=packed.shape[0]; D=packed.shape[1]//3; np_=D//128
    spec=lambda off: pl.BlockSpec((L,128),lambda p,off=off:(0,off+p))
    return pl.pallas_call(functools.partial(bwd_kernel,tq=tq),
        grid=(np_,),
        in_specs=[pl.BlockSpec(memory_space=pltpu.SMEM),spec(0),spec(np_),spec(2*np_),spec(0),spec(0),pl.BlockSpec((L,128),lambda p:(0,0))],
        out_specs=[spec(0)]*3,
        out_shape=[jax.ShapeDtypeStruct((L,D),BF)]*3,
        compiler_params=pltpu.CompilerParams(dimension_semantics=("arbitrary",),vmem_limit_bytes=60*2**20),
    )(lengths,packed,packed,packed,do,of,lse)

ISQ2=0.7071067811865476; ISQ2PI=0.3989422804014327
def gelu_both(x):
    phi=0.5+0.5*lax.erf(x*ISQ2)
    g=x*phi
    dg=phi+x*(jnp.exp2((x*x)*(-0.5*LOG2E))*ISQ2PI)
    return g,dg
NN=(((1,),(0,)),((),())); NT=(((1,),(1,)),((),())); TN=(((0,),(0,)),((),()))
def dotf(a,b,dn): return lax.dot_general(a,b,dn,preferred_element_type=F32)
def mlp_kernel(sec_ref, br_ref, win_ref, wout_ref, hid_ref, sg_ref, din_ref, dout_ref, act_s, eg_s, *, tr):
    j=pl.program_id(0)
    L=sec_ref.shape[0]
    win=win_ref[0]; wout=wout_ref[0]
    def row(i,_):
        sl=pl.ds(pl.multiple_of(i*tr,tr),tr)
        e=dotf(sec_ref[sl,:],win,NN)
        ag=dotf(br_ref[sl,:],wout,NN)
        g,dg=gelu_both(e)
        act=g.astype(BF); eg=(ag*dg).astype(BF)
        act_s[sl,:]=act; eg_s[sl,:]=eg
        h=dotf(act,wout,NT); s=dotf(eg,win,NT)
        @pl.when(j==0)
        def _():
            hid_ref[sl,:]=h; sg_ref[sl,:]=s
        @pl.when(j>0)
        def _():
            hid_ref[sl,:]+=h; sg_ref[sl,:]+=s
        return 0
    lax.fori_loop(0,L//tr,row,0)
    din_ref[0]=dotf(sec_ref[...],eg_s[...],TN).astype(din_ref.dtype)
    dout_ref[0]=dotf(br_ref[...],act_s[...],TN).astype(dout_ref.dtype)
def mlp(sec,br,win,wout,tr=256,gdt=BF):
    L,D=sec.shape; M,_,Fb=win.shape
    full=pl.BlockSpec((L,D),lambda j:(0,0)); blk=pl.BlockSpec((1,D,Fb),lambda j:(j,0,0))
    return pl.pallas_call(functools.partial(mlp_kernel,tr=tr),grid=(M,),
        in_specs=[full,full,blk,blk],out_specs=[full,full,blk,blk],
        out_shape=[jax.ShapeDtypeStruct((L,D),F32)]*2+[jax.ShapeDtypeStruct((M,D,Fb),gdt)]*2,
        scratch_shapes=[pltpu.VMEM((L,Fb),BF)]*2,
        compiler_params=pltpu.CompilerParams(dimension_semantics=("arbitrary",),vmem_limit_bytes=60*2**20))(sec,br,win,wout)

ALL = ("dp", "mp")
WIRE = ("mp", "dp")


def norm_stats(v):
    centre = v - jnp.mean(v, axis=-1, keepdims=True)
    r = lax.rsqrt(jnp.mean(centre * centre, axis=-1, keepdims=True) + 1e-06)
    return centre * r, r


def norm_pull(e, xhat, r, g):
    y = e * g
    back = r * (y - jnp.mean(y, axis=-1, keepdims=True) - xhat * jnp.mean(y * xhat, axis=-1, keepdims=True))
    return back, jnp.sum(e * xhat, axis=0), jnp.sum(e, axis=0)


def per_device(inputs, lengths, attn_qkv, attn_proj, mlp_in, mlp_out, norm_gain, norm_bias, cotangent):
    n_dp, n_mp = lax.axis_size("dp"), lax.axis_size("mp")
    n = n_dp * n_mp
    slots, width = inputs.shape
    rows = attn_qkv.shape[1]
    norms = jnp.concatenate([norm_gain[0], norm_bias[0]], axis=0).reshape(1, 4 * rows)
    norms = jnp.pad(norms, ((0, 0), (0, 3 * width - 4 * rows)))
    first = lax.all_gather(jnp.concatenate([attn_qkv[0], norms], axis=0), ALL, axis=0)
    second_part = jnp.concatenate([mlp_in[0].reshape(-1, 256), mlp_out[0].T.reshape(-1, 256)], axis=0)
    rest = lax.all_gather(second_part, WIRE, axis=0)
    proj_w = lax.all_gather(attn_proj[0], ALL, axis=0, tiled=True)
    qkv_w = first[:, :rows].reshape(width, 3 * width)
    params = first[:, rows, : 4 * rows].reshape(n, 4, rows).transpose(1, 0, 2).reshape(4, width).astype(F32)
    block = mlp_in.shape[2]
    win, wout = rest.reshape(n, 2, -1, block).transpose(1, 0, 2, 3).reshape(2, n_mp, width, block)

    hidden = inputs.astype(F32)
    xhat0, r0 = norm_stats(hidden)
    normed = (xhat0 * params[0] + params[2]).astype(BF)
    packed = jnp.dot(normed, qkv_w, preferred_element_type=F32).astype(BF)
    mixed, mixed_wide, logsum = att_fwd(lengths, packed, tq=min(512, slots))
    middle = hidden + jnp.dot(mixed, proj_w, preferred_element_type=F32)
    xhat1, r1 = norm_stats(middle)
    second = (xhat1 * params[1] + params[3]).astype(BF)
    valid = lax.iota(jnp.int32, slots) < lengths[0]
    branch = jnp.where(valid[:, None], cotangent, jnp.zeros_like(cotangent))
    mlp_sum, second_grad, in_grad, out_grad = mlp(second, branch, win, wout, tr=min(512, slots))
    outputs = (middle + mlp_sum).astype(BF)
    both = jnp.stack([in_grad, out_grad]).reshape(2, n, -1, block).transpose(1, 0, 2, 3)
    both = lax.psum_scatter(both, WIRE, scatter_dimension=0, tiled=False)
    part, gain1, bias1 = norm_pull(second_grad, xhat1, r1, params[1])
    middle_grad = branch.astype(F32) + part
    attn_low = middle_grad.astype(BF)
    proj_grad = lax.dot_general(mixed, attn_low, TN, preferred_element_type=F32).astype(BF)
    mixed_grad = lax.dot_general(attn_low, proj_w, NT, preferred_element_type=F32).astype(BF)
    packed_grad = jnp.concatenate(att_bwd(lengths, packed, mixed_grad, mixed_wide, logsum), axis=1)
    qkv_grad = lax.dot_general(normed, packed_grad, TN, preferred_element_type=F32).astype(BF)
    tail = jnp.concatenate([qkv_grad, proj_grad], axis=1).reshape(n, rows, 4 * width)
    tail = lax.psum_scatter(tail, ALL, scatter_dimension=0, tiled=False)
    normed_grad = lax.dot_general(packed_grad, qkv_w, NT, preferred_element_type=F32)
    part, gain0, bias0 = norm_pull(normed_grad, xhat0, r0, params[0])
    input_grad = middle_grad + part
    norm_grads = lax.psum(jnp.stack([gain0, gain1, bias0, bias1]), ALL)
    at = (lax.axis_index("dp") * n_mp + lax.axis_index("mp")) * rows
    mine = lax.dynamic_slice(norm_grads, (0, at), (4, rows))
    return (
        outputs,
        input_grad,
        tail[None, :, : 3 * width].astype(F32),
        tail[None, :, 3 * width :].astype(F32),
        both[0].astype(F32)[None],
        both[1].astype(F32).T[None],
        mine[None, :2],
        mine[None, 2:],
    )


def solution(mesh):
    wide = P(ALL, None)
    return jax.shard_map(
        per_device,
        mesh=mesh,
        in_specs=(wide, P(ALL), P(None, ALL, None), P(None, ALL, None), P(None, "dp", "mp"), P(None, "mp", "dp"),
                  P(None, None, ALL), P(None, None, ALL), wide),
        out_specs=(wide, wide, P(None, ALL, None), P(None, ALL, None), P(None, "dp", "mp"), P(None, "mp", "dp"),
                   P(None, None, ALL), P(None, None, ALL)),
        check_vma=False,
    )
```

time: 949 us -> 600 us (0.63)
  matrix products: 297 us -> 27.9 us
  Pallas kernels: 0 us -> 101 us
  blocking collectives: 125 us -> 39.7 us
  other arithmetic: 91 us -> 38.1 us
  local copies, waits for them, and re-layouts: 80.9 us -> 34.7 us
  waiting for transfers between devices: 328 us -> 342 us
    dot_general x26 -> x6, matrix products: 297 us -> 27.9 us  [the longest x1 9.53 us: per_device(): lax.dot_general(packed_grad, qkv_w, NT, preferred_element_type=F32)]
    all_gather x4 -> x3, waiting for transfers between devices: 0.05 us -> 159 us  [the longest x1 78.5 us: per_device(): rest = lax.all_gather(second_part, WIRE, axis=0)]
    all_gather x8 -> x0, blocking collectives: 113 us -> none  [the longest x1 18.5 us: collect(): lax.all_gather(qkv_part, 'mp', axis=0, tiled=True)]
    pallas_call x0 -> x3, Pallas kernels: none -> 101 us  [the longest x1 39.6 us: att_bwd(): pl.pallas_call(functools.partial(bwd_kernel, tq=tq), grid=(np_,), in_spec...]
    reduce_scatter x8 -> x2, waiting for transfers between devices: 277 us -> 182 us  [the longest x1 139 us: per_device(): both = lax.psum_scatter(both, WIRE, scatter_dimension=0, tiled=False)]
    unnamed x16 -> x5, waiting for transfers between devices: 51.5 us -> 0.76 us
    psum x0 -> x1, blocking collectives: none -> 39.7 us  [per_device(): norm_grads = lax.psum(jnp.stack([gain0, gain1, bias0, bias1]), ALL)]
    convert_element_type x5 -> x4, other arithmetic: 44.3 us -> 5.59 us  [the longest x1 1.7 us: per_device(): second = (xhat1 * params[1] + params[3]).astype(BF)]
  transfers between devices with their start and end apart: 14 -> 5, of which waited for: 9 -> 5; matrix products, arithmetic and copies ran while one was open for 43% -> 8% of each run, Pallas kernels for 0% -> 4%
where the time goes in v1:
time: 600 us; the launch traced here: 599 us
  waiting for transfers between devices  342 us (57%)
  Pallas kernels  101 us (17%)
  blocking collectives  39.7 us (7%)
  other arithmetic  38.1 us (6%)
  local copies, waits for them, and re-layouts  34.7 us (6%)
  matrix products  27.9 us (5%)
  between operations  14.7 us (2%)
    reduce_scatter x1, waiting for transfers between devices, per_device(): both = lax.psum_scatter(both, WIRE, scatter_dimension=0, tiled=False)  139 us
    all_gather x1, waiting for transfers between devices, per_device(): rest = lax.all_gather(second_part, WIRE, axis=0)  78.5 us
    all_gather x1, waiting for transfers between devices, per_device(): lax.all_gather(jnp.concatenate([attn_qkv[0], norms], axis=0), ALL, axis=0)  60 us
    reduce_scatter x1, waiting for transfers between devices, per_device(): tail = lax.psum_scatter(tail, ALL, scatter_dimension=0, tiled=False)  43.2 us
    psum x1, blocking collectives, per_device(): norm_grads = lax.psum(jnp.stack([gain0, gain1, bias0, bias1]), ALL)  39.7 us
    pallas_call x1, Pallas kernels, att_bwd(): pl.pallas_call(functools.partial(bwd_kernel, tq=tq), grid=(np_,), in_spec...  39.6 us
    pallas_call x1, Pallas kernels, mlp(): pl.pallas_call(functools.partial(mlp_kernel, tr=tr), grid=(M,), in_specs=...  38.6 us
    pallas_call x1, Pallas kernels, att_fwd(): pl.pallas_call(functools.partial(fwd_kernel, tq=tq, npair=np_), grid=(np_...  23.3 us
  transfers between devices with their start and end apart: 5, of which 5 were waited for; matrix products, arithmetic and copies ran while one was open for 8% of the time, Pallas kernels for 4%

profile of v1, /device:TPU:0, one launch (start us, length us, event | category | flops | bytes accessed | tf_op | source)
XLA Modules:
  0.0 598.9 jit_solution(9258154087863332636)
XLA Ops:
  7.2 0.0 all-gather.12.cloned.1.call-start
  7.2 0.8 pad_maximum_fusion.3
  8.1 0.1 reshape.119
  8.2 1.6 fusion.20
  9.7 0.0 all-gather.12.cloned.1.call-update
  9.7 0.0 all-gather.8.cloned.1.call-start
  9.8 0.7 all-gather.8.cloned.1.call-update
  10.5 0.0 all-gather.10.cloned.1.call-start
  10.5 1.0 reshape.121
  11.5 1.0 reshape_squeeze.4
  12.5 0.7 pad_maximum_fusion.1
  13.3 0.0 all-gather.10.cloned.1.call-update
  13.3 0.0 reduce-scatter.3.cloned.1.call-start
  14.0 1.7 convert_reduce_fusion
  15.7 0.6 fusion.13
  16.3 1.3 broadcast_select_fusion.br_ref
  17.7 60.0 %all-gather.12.cloned.1.call-done = bf16[32,25,2304]{2,1,0:T(8,128)(2,1)} async-done(((bf16[1,25,2304]{2,1,0:T(8,128)(2,1)}), bf16[32,25,2304]{2,1,0:T(8,128)(2,1)}) %all-gather.12.cloned.1.call-update) | async-done | bytes 3686416 | tf_op jit(solution)/shard_map/all_gather | solution.py:184
  77.7 0.9 fusion.24
  78.6 0.1 reshape.128
  78.7 0.2 slice_reduce_fusion.1
  78.9 0.1 mul.103
  78.9 0.1 add.63
  79.0 2.2 slice.61
  81.3 1.9 copy-done.6
  83.2 6.0 convolution_convert_fusion.q_ref.k_ref.v_ref
  89.1 23.3 %shard_map.152 = (bf16[1024,768]{1,0:T(8,128)(2,1)}, f32[1024,768]{1,0:T(8,128)}, f32[1024,128]{1,0:T(8,128)}) custom-call(s32[1]{0:T(128)} %copy.33.len_ref, bf16[1024,2304]{1,0:T(8,128)(2,1)} %convolution_convert_fusion.q_ref.k_ref.v_ref, bf16[1024,2304]{1,0:T(8,128)(2,1)} %convolution_convert_fusion.q_ref.k_ref.v_ref, ...), custom_call_target="tpu_custom_call" | custom-call | tf_op jit(solution)/shard_map/pallas_call | solution.py:60
  112.4 0.1 mul.109
  112.5 0.1 add.68
  112.6 20.8 %all-gather.8.cloned.1.call-done = bf16[1,768,768]{2,1,0:T(8,128)(2,1)} async-done(((bf16[1,24,768]{2,1,0:T(8,128)(2,1)}), bf16[1,768,768]{2,1,0:T(8,128)(2,1)}) %all-gather.8.cloned.1.call-update) | async-done | bytes 1179664 | tf_op jit(solution)/shard_map/all_gather | solution.py:187
  133.4 3.8 fusion.28
  137.2 0.5 multiply_reduce_fusion.2
  137.7 1.7 add_convert_fusion.1.sec_ref
  139.4 78.5 %all-gather.10.cloned.1.call-done = bf16[18432,256]{1,0:T(8,128)(2,1)} async-done(((bf16[576,256]{1,0:T(8,128)(2,1)}), bf16[18432,256]{1,0:T(8,128)(2,1)}) %all-gather.10.cloned.1.call-update) | async-done | bytes 9437200 | tf_op jit(solution)/shard_map/all_gather | solution.py:186
  217.9 15.1 %reshape.122 = bf16[32,2,96,768]{3,2,1,0:T(8,128)(2,1)} reshape(bf16[18432,256]{1,0:T(8,128)(2,1)} %all-gather.10.cloned.1.call-done) | data formatting | bytes 18874368 | tf_op jit(solution)/shard_map/reshape | solution.py:191
  233.0 8.0 %fusion.27 = (bf16[1,32,96,768]{3,2,0,1:T(8,128)(2,1)}, bf16[1,32,96,768]{3,2,0,1:T(8,128)(2,1)}) fusion(bf16[2,32,96,768]{3,2,0,1:T(8,128)(2,1)} %bitcast.66), kind=kLoop, calls=%fused_computation.73 | loop fusion | bytes 18874368 | tf_op jit(solution)/shard_map/unstack | solution.py:191
  241.0 38.6 %shard_map.153 = (f32[1024,768]{1,0:T(8,128)}, f32[1024,768]{1,0:T(8,128)}, bf16[4,768,768]{2,1,0:T(8,128)(2,1)}, bf16[4,768,768]{2,1,0:T(8,128)(2,1)}) custom-call(bf16[1024,768]{1,0:T(8,128)(2,1)} %add_convert_fusion.1.sec_ref, bf16[1024,768]{1,0:T(8,128)(2,1)} %broadcast_select_fusion.br_ref, bf16[4,768,768]{2,1,0:T(8,128)(2,1)} %bitcast.69, ...), custom_call_target="tpu_custom_call" | custom-call | tf_op jit(solution)/shard_map/pallas_call | solution.py:155
  279.6 3.1 multiply_reduce_fusion
  282.7 0.1 copy-done.5
  282.9 4.6 multiply_add_fusion
  287.5 1.5 convolution_convert_fusion.3
  289.0 0.1 copy-done.2
  289.1 0.5 copy-done.11
  289.6 2.6 convolution_convert_fusion.2.do_ref
  292.2 39.6 %shard_map.154 = (bf16[1024,768]{1,0:T(8,128)(2,1)}, bf16[1024,768]{1,0:T(8,128)(2,1)}, bf16[1024,768]{1,0:T(8,128)(2,1)}) custom-call(s32[1]{0:T(128)} %copy.33.len_ref, bf16[1024,2304]{1,0:T(8,128)(2,1)} %convolution_convert_fusion.q_ref.k_ref.v_ref, bf16[1024,2304]{1,0:T(8,128)(2,1)} %convolution_convert_fusion.q_ref.k_ref.v_ref, ...), custom_call_target="tpu_custom_call" | custom-call | tf_op jit(solution)/shard_map/pallas_call | solution.py:114
  331.8 1.7 constant_dynamic-update-slice_fusion.2
  333.5 0.2 copy-done.8
  333.7 0.1 constant_dynamic-update-slice_fusion.1
  333.8 0.4 copy-done.7
  334.1 0.1 constant_dynamic-update-slice_fusion
  334.3 0.9 copy-done.1
  335.2 4.6 convolution_convert_fusion.1
  339.8 2.8 pad_maximum_fusion
  342.6 0.3 reduce-scatter.5.cloned.1.call-start
  342.9 8.3 %maximum_bitcast_fusion = bf16[32,2,96,768]{3,2,1,0:T(8,128)(2,1)} fusion(bf16[1,32,96,768]{3,2,0,1:T(8,128)(2,1)} %bitcast.71, bf16[1,32,96,768]{3,2,0,1:T(8,128)(2,1)} %bitcast.70), kind=kLoop, calls=%fused_computation | loop fusion | flops 4718592 | bytes 18874368 | tf_op jit(solution)/shard_map/transpose | solution.py:205
  351.2 9.5 %fusion.12 = (f32[768]{0:T(1024)S(1)}, f32[1024]{0:T(1024)S(1)}, f32[1024]{0:T(1024)S(1)}, f32[768]{0:T(1024)S(1)}, f32[1024,768]{1,0:T(8,128)}) fusion(bf16[1024,768]{1,0:T(8,128)(2,1)S(1)} %copy-done.1, f32[1024]{0:T(1024)S(1)} %add_rsqrt_fusion.1, f32[1024]{0:T(1024)S(1)} %broadcast_multiply_fusion.5, f32[768]{0:T(1024)S(1)} %mul.103, ...), kind=kOutput, calls=%fused_computation.19 | convolution fusion | flops 3631739392 | bytes 13001728 | tf_op jit(solution)/shard_map/dot_general | solution.py:216
  360.8 39.7 %psum.7 = f32[4,768]{1,0:T(4,128)S(1)} all-reduce(f32[4,768]{1,0:T(4,128)S(1)} %pad_maximum_fusion.2), channel_id=1, replica_groups=mesh['dp'=8,'mp'=4] {'dp','mp'}, use_global_device_ids=true, to_apply=%region_14.15 | all-reduce | flops 3072 | bytes 24576 | tf_op jit(solution)/shard_map/psum | solution.py:219
  400.5 0.1 constant_dynamic-slice_fusion
  400.6 0.6 slice_bitcast_fusion.4
  401.2 4.6 fusion.11
  405.8 43.2 %reduce-scatter.3.cloned.1.call-done = bf16[1,24,3072]{2,1,0:T(8,128)(2,1)} async-done(((bf16[32,24,3072]{2,1,0:T(8,128)(2,1)}), bf16[1,24,3072]{2,1,0:T(8,128)(2,1)}) %reduce-scatter.3.cloned.1.call-update) | async-done | bytes 147472 | tf_op jit(solution)/shard_map/reduce_scatter | solution.py:215
  449.0 1.4 fusion.23
  450.4 1.6 fusion.22
  452.0 138.6 %reduce-scatter.5.cloned.1.call-done = bf16[1,2,96,768]{3,2,1,0:T(8,128)(2,1)} async-done(((bf16[32,2,96,768]{3,2,1,0:T(8,128)(2,1)}), bf16[1,2,96,768]{3,2,1,0:T(8,128)(2,1)}) %reduce-scatter.5.cloned.1.call-update) | async-done | bytes 294928 | tf_op jit(solution)/shard_map/reduce_scatter | solution.py:206
  590.5 1.8 convert_bitcast_fusion
  (32 shorter events, 0.1 us)
Async XLA Ops:
  7.2 8.5 %copy-start = (bf16[1024,768]{1,0:T(8,128)(2,1)S(1)}, bf16[1024,768]{1,0:T(8,128)(2,1)}, u32[]{:S(2)}) copy-start(bf16[1024,768]{1,0:T(8,128)(2,1)} %param.9) | copy-start | bytes 4718596
  7.2 9.1 %copy-start.4 = (bf16[1024,768]{1,0:T(8,128)(2,1)S(1)}, bf16[1024,768]{1,0:T(8,128)(2,1)}, u32[]{:S(2)}) copy-start(bf16[1024,768]{1,0:T(8,128)(2,1)} %param.17) | copy-start | bytes 4718596
  7.2 70.5 %all-gather.12.cloned.1.call-start = ((), (), s32[]{:S(2)}) async-start(), calls=%async_computation.6 | async-start | bytes 4866048 | tf_op jit(solution)/shard_map/all_gather | solution.py:184
  9.7 123.7 %all-gather.8.cloned.1.call-start = ((), (), s32[]{:S(2)}) async-start(), calls=%async_computation.4 | async-start | bytes 1216512 | tf_op jit(solution)/shard_map/all_gather | solution.py:187
  10.5 207.4 %all-gather.10.cloned.1.call-start = ((), (), s32[]{:S(2)}) async-start(), calls=%async_computation.5 | async-start | bytes 9732096 | tf_op jit(solution)/shard_map/all_gather | solution.py:186
  13.3 435.7 %reduce-scatter.3.cloned.1.call-start = ((), (), s32[]{:S(2)}) async-start(), calls=%async_computation.2 | async-start | bytes 4866048 | tf_op jit(solution)/shard_map/reduce_scatter | solution.py:215
  81.3 1.9 copy-start.6
  279.6 3.1 copy-start.3
  279.6 3.3 copy-start.5
  282.9 4.6 copy-start.10
  287.5 1.6 copy-start.2
  287.5 2.1 copy-start.11
  331.8 1.9 copy-start.8
  331.8 2.3 copy-start.7
  333.7 1.5 copy-start.1
  335.2 4.6 copy-start.9
  342.6 247.9 %reduce-scatter.5.cloned.1.call-start = ((), (), s32[]{:S(2)}) async-start(), calls=%async_computation.3 | async-start | bytes 9732096 | tf_op jit(solution)/shard_map/reduce_scatter | solution.py:206
Sparse Core Ops, SparseCore 0:
  11.4 66.2 all-gather.11
  80.5 52.8 all-gather.7
  136.9 80.9 all-gather.9
  342.7 106.1 reduce-scatter.2
  455.7 134.7 reduce-scatter.4
